TPU v7x, 128 devices: a whole 4x4x4 slice. The times are simulated.
128 devices in a mesh: dom: 32 (over x_lo, z, y), rep: 4 (over x_hi, core).
Axes of the slice: x: 4 (x_hi: 2, x_lo: 2; x = x_hi * 2 + x_lo), y: 4, z: 4, core: 2. Of those that a mesh axis runs over, the one named last changes fastest.
Arguments:
- features: bfloat16 [49152, 256], P('dom'), may hold values from -6 to 6
- tile_weights: bfloat16 [32, 4, 8, 88, 128, 128], P('dom', 'rep'), may hold values from 0 to 0.0115356445
- tile_rows: int32 [32, 4, 8, 88], P('dom', 'rep'), may hold values from 0 to 11, as said below
- tile_cols: int32 [32, 4, 8, 88], P('dom', 'rep'), may hold values from 0 to 11, as said below
- tile_counts: int32 [32, 4, 8], P('dom', 'rep'), may hold values from 1 to 88, as said below
- weight_self: bfloat16 [256, 256], replicated, may hold values from -0.375 to 0.375
- weight_neigh: bfloat16 [256, 256], replicated, may hold values from -0.375 to 0.375
- cotangent: bfloat16 [49152, 256], P(('dom', 'rep')), may hold values from -0.026977539 to 0.026977539
Outputs:
- out: bfloat16 [49152, 256], P(('dom', 'rep'))
- grad_self: float32 [256, 256], replicated
- grad_neigh: float32 [256, 256], replicated
Inputs may be any that keep to these rules, and one draw needn't show every extreme that they name: For each p, r, s the first tile_counts[p, r, s] slots name distinct pairs (tile_rows, tile_cols); slots from tile_counts[p, r, s] on are unused. `tile_cols`: see tile_rows. `tile_counts`: some device fills all 88 slots of some column step.
All inputs are finite; a program needn't handle non-finite values.
Results may differ from a plain program's by a relative error of at most 0.0052.
Values may be sent and summed in bfloat16 or wider, within the bound.
A program may use at most 128 MiB of HBM per device.

v0:
```python
import jax
import jax.numpy as jnp
from jax import lax
from jax.sharding import PartitionSpec as P


def passed_along(block, axis, distance):
    devices = range(lax.axis_size(axis))
    route = [((i - distance) % len(devices), i) for i in devices]
    return lax.ppermute(block, axis, route)


def step_terms(feature_block, weights_dev, rows_dev, cols_dev, counts_dev, column_step):
    weights_now = lax.dynamic_index_in_dim(weights_dev, column_step, 0, keepdims=False)
    row_index = lax.dynamic_index_in_dim(rows_dev, column_step, 0, keepdims=False)
    col_index = lax.dynamic_index_in_dim(cols_dev, column_step, 0, keepdims=False)
    live_total = lax.dynamic_index_in_dim(counts_dev, column_step, 0, keepdims=False)
    slot_total = weights_now.shape[0]
    tile_side = weights_now.shape[1]
    width = feature_block.shape[1]
    row_tiles = feature_block.shape[0] // tile_side
    flat_block = feature_block.reshape(row_tiles, tile_side * width)
    tile_ids = jnp.arange(row_tiles, dtype=jnp.int32)
    select = (col_index[:, None] == tile_ids[None, :]).astype(jnp.bfloat16)
    picked = jnp.dot(select, flat_block, preferred_element_type=jnp.float32).astype(jnp.bfloat16)
    picked = picked.reshape(slot_total, tile_side, width)
    product = jnp.einsum("kij,kjf->kif", weights_now, picked, preferred_element_type=jnp.float32)
    live_slots = jnp.arange(slot_total, dtype=jnp.int32) < live_total
    placing = ((row_index[None, :] == tile_ids[:, None]) & live_slots[None, :]).astype(jnp.float32)
    summed = jnp.dot(
        placing,
        product.reshape(slot_total, tile_side * width),
        precision=lax.Precision.HIGHEST,
        preferred_element_type=jnp.float32,
    )
    return summed.reshape(feature_block.shape[0], width)


def rotate(feature_block, steps_per_group, offset, direction_sign):
    replica = lax.axis_index("rep")
    bit_total = (lax.axis_size("rep") - 1).bit_length()
    domain = lax.axis_size("dom")
    moves = []
    moves.append((offset % domain, -1))
    for bit_number in range(bit_total):
        moves.append((direction_sign * steps_per_group * (1 << bit_number) % domain, bit_number))
    for amount, bit_number in moves:
        shifted = passed_along(feature_block, "dom", amount)
        if bit_number < 0:
            feature_block = shifted
        else:
            flag = replica >> bit_number & 1 == 1
            feature_block = jnp.where(flag, shifted, feature_block)
    return feature_block


def move_up(feature_block):
    return passed_along(feature_block, "dom", -1)


def on_device(
    features, tile_weights, tile_rows, tile_cols, tile_counts, weight_self, weight_neigh, cotangent
):
    weights_dev = tile_weights[0, 0]
    rows_dev = tile_rows[0, 0]
    cols_dev = tile_cols[0, 0]
    counts_dev = tile_counts[0, 0]
    steps_per_group = weights_dev.shape[0]
    middle = steps_per_group // 2

    def contribution(feature_block, column_step):
        return step_terms(feature_block, weights_dev, rows_dev, cols_dev, counts_dev, column_step)

    empty = jnp.zeros(features.shape, jnp.float32)
    begin = rotate(features, steps_per_group, middle, -1)

    def turn_one(turn_index, carry):
        current, partial_value = carry
        partial_value = partial_value + contribution(current, turn_index)
        return (move_up(current), partial_value)

    current, partial_value = lax.fori_loop(0, steps_per_group - 1, turn_one, (begin, empty))
    partial_value = partial_value + contribution(current, steps_per_group - 1)
    aggregate = lax.psum_scatter(partial_value, "rep", scatter_dimension=0, tiled=True).astype(
        jnp.bfloat16
    )
    quarter = features.shape[0] // lax.axis_size("rep")
    own_rows = lax.dynamic_slice_in_dim(features, lax.axis_index("rep") * quarter, quarter, 0)
    pre = jnp.dot(own_rows, weight_self, preferred_element_type=jnp.float32)
    pre = pre + jnp.dot(aggregate, weight_neigh, preferred_element_type=jnp.float32)
    output = jax.nn.silu(pre).astype(jnp.bfloat16)
    sigmoid = jax.nn.sigmoid(pre)
    slope = (cotangent.astype(jnp.float32) * sigmoid * (1.0 + pre * (1.0 - sigmoid))).astype(
        jnp.bfloat16
    )
    self_term = jnp.einsum("nf,ng->fg", own_rows, slope, preferred_element_type=jnp.float32)
    neigh_term = jnp.einsum("nf,ng->fg", aggregate, slope, preferred_element_type=jnp.float32)
    grad_self, grad_neigh = lax.psum((self_term, neigh_term), ("dom", "rep"))
    return (output, grad_self, grad_neigh)


def solution(mesh):
    return jax.shard_map(
        on_device,
        mesh=mesh,
        in_specs=(
            P("dom", None),
            P("dom", "rep", None, None, None, None),
            P("dom", "rep", None, None),
            P("dom", "rep", None, None),
            P("dom", "rep", None),
            P(),
            P(),
            P(("dom", "rep"), None),
        ),
        out_specs=(P(("dom", "rep"), None), P(), P()),
        check_vma=False,
    )
```

profile of v0, /device:TPU:1, one launch (start us, length us, event | category | flops | bytes accessed | tf_op | source)
XLA Modules:
  0.0 608.2 jit_solution(17502834930815847477)
XLA Ops:
  9.7 20.5 %collective-permute-done.1 = bf16[1536,256]{1,0:T(8,128)(2,1)S(1)} collective-permute-done((bf16[1536,256]{1,0:T(8,128)(2,1)}, bf16[1536,256]{1,0:T(8,128)(2,1)S(1)}, u32[]{:S(2)}, u32[]{:S(2)}) %collective-permute-start.1) | collective-permute-done | bytes 786464 | tf_op jit(solution)/shard_map/ppermute | solution.py:10
  31.3 18.3 %collective-permute-done.2 = bf16[1536,256]{1,0:T(8,128)(2,1)S(1)} collective-permute-done((bf16[1536,256]{1,0:T(8,128)(2,1)S(1)}, bf16[1536,256]{1,0:T(8,128)(2,1)S(1)}, u32[]{:S(2)}, u32[]{:S(2)}) %collective-permute-start.2) | collective-permute-done | bytes 786464 | tf_op jit(solution)/shard_map/ppermute | solution.py:10
  53.1 13.7 %collective-permute-done.3 = bf16[1536,256]{1,0:T(8,128)(2,1)S(1)} collective-permute-done((bf16[1536,256]{1,0:T(8,128)(2,1)S(1)}, bf16[1536,256]{1,0:T(8,128)(2,1)S(1)}, u32[]{:S(2)}, u32[]{:S(2)}) %collective-permute-start.3) | collective-permute-done | bytes 786464 | tf_op jit(solution)/shard_map/ppermute | solution.py:10
  67.8 301.9 %while.16 = (s32[]{:T(128)}, bf16[1536,256]{1,0:T(8,128)(2,1)}, f32[1536,256]{1,0:T(8,128)}, s32[8,88]{1,0:T(8,128)}, s32[8]{0:T(128)}, /*index=5*/bf16[8,88,128...) while((s32[]{:T(128)}, bf16[1536,256]{1,0:T(8,128)(2,1)}, f32[1536,256]{1,0:T(8,128)}, ...), condition=%wide.region_1.2_spmd.clone, body=%wide.region_0.1_spmd.clone.sunk | while | flops 1226312832 | bytes 88607792 | solution.py:82
  69.0 3.9 collective-permute-start
  77.4 7.8 %fusion.53 = f32[88,128,256]{2,1,0:T(8,128)} fusion(bf16[88,128,256]{2,1,0:T(8,128)(2,1)S(1)} %bitcast.64, bf16[8,88,128,128]{3,2,1,0:T(8,128)(2,1)} %get-tuple-element.244, s32[]{:T(128)} %get-tuple-element.230), kind=kOutput, calls=%fused_computation.1.clone.1 | convolution fusion | flops 738197504 | bytes 20185600 | tf_op jit(solution)/shard_map/while/body/eval_jaxpr/kij,kjf->kif/dot_general | solution.py:27
  85.2 16.1 %copy.23 = f32[11,8,128,256]{3,1,2,0:T(8,128)} copy(f32[11,8,128,256]{3,2,1,0:T(8,128)} %bitcast.62) | data formatting | bytes 23068672 | tf_op jit(solution)/shard_map/while
  102.5 6.7 %fusion.54 = f32[12,32768]{1,0:T(8,128)S(1)} fusion(f32[88,32768]{1,0:T(8,128)} %bitcast.61, s32[88]{0:T(128)S(1)} %get-tuple-element.220, pred[88]{0:T(512)(128)(4,1)S(1)} %iota_compare_fusion.11), kind=kOutput, calls=%fused_computation.9.clone.1 | convolution fusion | flops 415238208 | bytes 13107640 | tf_op jit(solution)/shard_map/while/body/eval_jaxpr/dot_general | solution.py:30
  119.4 7.8 %fusion.53 = f32[88,128,256]{2,1,0:T(8,128)} fusion(bf16[88,128,256]{2,1,0:T(8,128)(2,1)S(1)} %bitcast.64, bf16[8,88,128,128]{3,2,1,0:T(8,128)(2,1)} %get-tuple-element.244, s32[]{:T(128)} %get-tuple-element.230), kind=kOutput, calls=%fused_computation.1.clone.1 | convolution fusion | flops 738197504 | bytes 20185600 | tf_op jit(solution)/shard_map/while/body/eval_jaxpr/kij,kjf->kif/dot_general | solution.py:27
  127.2 16.1 %copy.23 = f32[11,8,128,256]{3,1,2,0:T(8,128)} copy(f32[11,8,128,256]{3,2,1,0:T(8,128)} %bitcast.62) | data formatting | bytes 23068672 | tf_op jit(solution)/shard_map/while
  144.6 6.7 %fusion.54 = f32[12,32768]{1,0:T(8,128)S(1)} fusion(f32[88,32768]{1,0:T(8,128)} %bitcast.61, s32[88]{0:T(128)S(1)} %get-tuple-element.220, pred[88]{0:T(512)(128)(4,1)S(1)} %iota_compare_fusion.11), kind=kOutput, calls=%fused_computation.9.clone.1 | convolution fusion | flops 415238208 | bytes 13107640 | tf_op jit(solution)/shard_map/while/body/eval_jaxpr/dot_general | solution.py:30
  152.6 3.2 select_add_fusion.2
  161.7 7.8 %fusion.53 = f32[88,128,256]{2,1,0:T(8,128)} fusion(bf16[88,128,256]{2,1,0:T(8,128)(2,1)S(1)} %bitcast.64, bf16[8,88,128,128]{3,2,1,0:T(8,128)(2,1)} %get-tuple-element.244, s32[]{:T(128)} %get-tuple-element.230), kind=kOutput, calls=%fused_computation.1.clone.1 | convolution fusion | flops 738197504 | bytes 20185600 | tf_op jit(solution)/shard_map/while/body/eval_jaxpr/kij,kjf->kif/dot_general | solution.py:27
  169.4 16.1 %copy.23 = f32[11,8,128,256]{3,1,2,0:T(8,128)} copy(f32[11,8,128,256]{3,2,1,0:T(8,128)} %bitcast.62) | data formatting | bytes 23068672 | tf_op jit(solution)/shard_map/while
  186.8 6.7 %fusion.54 = f32[12,32768]{1,0:T(8,128)S(1)} fusion(f32[88,32768]{1,0:T(8,128)} %bitcast.61, s32[88]{0:T(128)S(1)} %get-tuple-element.220, pred[88]{0:T(512)(128)(4,1)S(1)} %iota_compare_fusion.11), kind=kOutput, calls=%fused_computation.9.clone.1 | convolution fusion | flops 415238208 | bytes 13107640 | tf_op jit(solution)/shard_map/while/body/eval_jaxpr/dot_general | solution.py:30
  203.9 7.8 %fusion.53 = f32[88,128,256]{2,1,0:T(8,128)} fusion(bf16[88,128,256]{2,1,0:T(8,128)(2,1)S(1)} %bitcast.64, bf16[8,88,128,128]{3,2,1,0:T(8,128)(2,1)} %get-tuple-element.244, s32[]{:T(128)} %get-tuple-element.230), kind=kOutput, calls=%fused_computation.1.clone.1 | convolution fusion | flops 738197504 | bytes 20185600 | tf_op jit(solution)/shard_map/while/body/eval_jaxpr/kij,kjf->kif/dot_general | solution.py:27
  211.7 16.1 %copy.23 = f32[11,8,128,256]{3,1,2,0:T(8,128)} copy(f32[11,8,128,256]{3,2,1,0:T(8,128)} %bitcast.62) | data formatting | bytes 23068672 | tf_op jit(solution)/shard_map/while
  229.0 6.7 %fusion.54 = f32[12,32768]{1,0:T(8,128)S(1)} fusion(f32[88,32768]{1,0:T(8,128)} %bitcast.61, s32[88]{0:T(128)S(1)} %get-tuple-element.220, pred[88]{0:T(512)(128)(4,1)S(1)} %iota_compare_fusion.11), kind=kOutput, calls=%fused_computation.9.clone.1 | convolution fusion | flops 415238208 | bytes 13107640 | tf_op jit(solution)/shard_map/while/body/eval_jaxpr/dot_general | solution.py:30
  248.5 7.8 %fusion.53 = f32[88,128,256]{2,1,0:T(8,128)} fusion(bf16[88,128,256]{2,1,0:T(8,128)(2,1)S(1)} %bitcast.64, bf16[8,88,128,128]{3,2,1,0:T(8,128)(2,1)} %get-tuple-element.244, s32[]{:T(128)} %get-tuple-element.230), kind=kOutput, calls=%fused_computation.1.clone.1 | convolution fusion | flops 738197504 | bytes 20185600 | tf_op jit(solution)/shard_map/while/body/eval_jaxpr/kij,kjf->kif/dot_general | solution.py:27
  256.3 16.1 %copy.23 = f32[11,8,128,256]{3,1,2,0:T(8,128)} copy(f32[11,8,128,256]{3,2,1,0:T(8,128)} %bitcast.62) | data formatting | bytes 23068672 | tf_op jit(solution)/shard_map/while
  273.7 6.7 %fusion.54 = f32[12,32768]{1,0:T(8,128)S(1)} fusion(f32[88,32768]{1,0:T(8,128)} %bitcast.61, s32[88]{0:T(128)S(1)} %get-tuple-element.220, pred[88]{0:T(512)(128)(4,1)S(1)} %iota_compare_fusion.11), kind=kOutput, calls=%fused_computation.9.clone.1 | convolution fusion | flops 415238208 | bytes 13107640 | tf_op jit(solution)/shard_map/while/body/eval_jaxpr/dot_general | solution.py:30
  291.0 7.8 %fusion.53 = f32[88,128,256]{2,1,0:T(8,128)} fusion(bf16[88,128,256]{2,1,0:T(8,128)(2,1)S(1)} %bitcast.64, bf16[8,88,128,128]{3,2,1,0:T(8,128)(2,1)} %get-tuple-element.244, s32[]{:T(128)} %get-tuple-element.230), kind=kOutput, calls=%fused_computation.1.clone.1 | convolution fusion | flops 738197504 | bytes 20185600 | tf_op jit(solution)/shard_map/while/body/eval_jaxpr/kij,kjf->kif/dot_general | solution.py:27
  298.8 16.1 %copy.23 = f32[11,8,128,256]{3,1,2,0:T(8,128)} copy(f32[11,8,128,256]{3,2,1,0:T(8,128)} %bitcast.62) | data formatting | bytes 23068672 | tf_op jit(solution)/shard_map/while
  316.2 6.7 %fusion.54 = f32[12,32768]{1,0:T(8,128)S(1)} fusion(f32[88,32768]{1,0:T(8,128)} %bitcast.61, s32[88]{0:T(128)S(1)} %get-tuple-element.220, pred[88]{0:T(512)(128)(4,1)S(1)} %iota_compare_fusion.11), kind=kOutput, calls=%fused_computation.9.clone.1 | convolution fusion | flops 415238208 | bytes 13107640 | tf_op jit(solution)/shard_map/while/body/eval_jaxpr/dot_general | solution.py:30
  333.3 7.8 %fusion.53 = f32[88,128,256]{2,1,0:T(8,128)} fusion(bf16[88,128,256]{2,1,0:T(8,128)(2,1)S(1)} %bitcast.64, bf16[8,88,128,128]{3,2,1,0:T(8,128)(2,1)} %get-tuple-element.244, s32[]{:T(128)} %get-tuple-element.230), kind=kOutput, calls=%fused_computation.1.clone.1 | convolution fusion | flops 738197504 | bytes 20185600 | tf_op jit(solution)/shard_map/while/body/eval_jaxpr/kij,kjf->kif/dot_general | solution.py:27
  341.1 16.1 %copy.23 = f32[11,8,128,256]{3,1,2,0:T(8,128)} copy(f32[11,8,128,256]{3,2,1,0:T(8,128)} %bitcast.62) | data formatting | bytes 23068672 | tf_op jit(solution)/shard_map/while
  358.4 6.7 %fusion.54 = f32[12,32768]{1,0:T(8,128)S(1)} fusion(f32[88,32768]{1,0:T(8,128)} %bitcast.61, s32[88]{0:T(128)S(1)} %get-tuple-element.220, pred[88]{0:T(512)(128)(4,1)S(1)} %iota_compare_fusion.11), kind=kOutput, calls=%fused_computation.9.clone.1 | convolution fusion | flops 415238208 | bytes 13107640 | tf_op jit(solution)/shard_map/while/body/eval_jaxpr/dot_general | solution.py:30
  374.5 8.6 %convolution_bitcast_fusion = f32[88,128,256]{1,2,0:T(8,128)} fusion(bf16[88,128,256]{2,1,0:T(8,128)(2,1)S(1)} %bitcast.68, bf16[1,1,8,88,128,128]{5,4,3,2,1,0:T(8,128)(2,1)} %bitcast.70), kind=kOutput, calls=%fused_computation.19 | convolution fusion | flops 738197504 | bytes 20185088 | tf_op jit(solution)/shard_map/kij,kjf->kif/dot_general | solution.py:27
  383.1 12.2 %copy.18 = f32[11,8,128,256]{3,1,2,0:T(8,128)} copy(f32[11,8,128,256]{2,3,1,0:T(8,128)} %bitcast.66) | data formatting | bytes 23068672
  395.3 8.2 %fusion.23 = f32[12,32768]{1,0:T(8,128)} fusion(f32[88,32768]{1,0:T(8,128)} %bitcast.65, s32[88]{0:T(128)S(1)} %slice_bitcast_fusion.1, pred[88]{0:T(512)(128)(4,1)S(1)} %iota_compare_fusion.7), kind=kOutput, calls=%fused_computation.39 | convolution fusion | flops 415238208 | bytes 13107640 | tf_op jit(solution)/shard_map/dot_general | solution.py:30
  407.9 37.6 %reduce-scatter.2.cloned.1.call-done = f32[384,256]{1,0:T(8,128)} async-done(((f32[1536,256]{1,0:T(8,128)}), f32[384,256]{1,0:T(8,128)}) %reduce-scatter.2.cloned.1.call-update) | async-done | bytes 393232 | tf_op jit(solution)/shard_map/reduce_scatter | solution.py:84
  451.5 146.5 %all-reduce.3.cloned.1.call-done = (f32[256,256]{1,0:T(8,128)}, f32[256,256]{1,0:T(8,128)}) async-done(((f32[256,256]{1,0:T(8,128)}, f32[256,256]{1,0:T(8,128)}), (f32[256,256]{1,0:T(8,128)}, f32[256,256]{1,0:T(8,128)})) %all-reduce.3.cloned.1.call-update) | async-done | bytes 524304 | tf_op jit(solution)/shard_map/psum | solution.py:98
  (120 shorter events, 106.8 us)
Async XLA Ops:
  7.2 438.4 %copy-start = (bf16[256,256]{1,0:T(8,128)(2,1)S(1)}, bf16[256,256]{1,0:T(8,128)(2,1)}, u32[]{:S(2)}) copy-start(bf16[256,256]{1,0:T(8,128)(2,1)} %param.16) | copy-start | bytes 393220
  7.2 438.4 %reduce-scatter.2.cloned.1.call-start = ((), (), s32[]{:S(2)}) async-start(), calls=%async_computation.1 | async-start | bytes 1966080 | tf_op jit(solution)/shard_map/reduce_scatter | solution.py:84
  7.2 23.0 %collective-permute-start.1 = (bf16[1536,256]{1,0:T(8,128)(2,1)}, bf16[1536,256]{1,0:T(8,128)(2,1)S(1)}, u32[]{:S(2)}, u32[]{:S(2)}) collective-permute-start(bf16[1536,256]{1,0:T(8,128)(2,1)} %param.10), channel_id=1, source_target_pairs={{112,0},{116,4},{120,8},{124,12},{0,16},{4,20},{8,24},{12,28},{16,... | collective-permute-start | bytes 2359304 | tf_op jit(solution)/shard_map/ppermute | solution.py:10
  30.3 19.4 %collective-permute-start.2 = (bf16[1536,256]{1,0:T(8,128)(2,1)S(1)}, bf16[1536,256]{1,0:T(8,128)(2,1)S(1)}, u32[]{:S(2)}, u32[]{:S(2)}) collective-permute-start(bf16[1536,256]{1,0:T(8,128)(2,1)S(1)} %collective-permute-done.1), channel_id=1, source_target_pairs={{32,0},{36,4},{40,8},{44,12},{48,16},{52,20},{56,24},{60,28},{64,3... | collective-permute-start | bytes 2359304 | tf_op jit(solution)/shard_map/ppermute | solution.py:10
  49.7 17.1 %collective-permute-start.3 = (bf16[1536,256]{1,0:T(8,128)(2,1)S(1)}, bf16[1536,256]{1,0:T(8,128)(2,1)S(1)}, u32[]{:S(2)}, u32[]{:S(2)}) collective-permute-start(bf16[1536,256]{1,0:T(8,128)(2,1)S(1)} %broadcast_select_fusion), channel_id=1, source_target_pairs={{64,0},{68,4},{72,8},{76,12},{80,16},{84,20},{88,24},{92,28},{96,3... | collective-permute-start | bytes 2359304 | tf_op jit(solution)/shard_map/ppermute | solution.py:10
  69.0 44.4 %collective-permute-start = (bf16[1536,256]{1,0:T(8,128)(2,1)S(1)}, bf16[1536,256]{1,0:T(8,128)(2,1)}, u32[]{:S(2)}, u32[]{:S(2)}) collective-permute-start(bf16[1536,256]{1,0:T(8,128)(2,1)S(1)} %copy.28), channel_id=1, source_target_pairs={{4,0},{8,4},{12,8},{16,12},{20,16},{24,20},{28,24},{32,28},{36,32}... | collective-permute-start | bytes 2359304 | tf_op jit(solution)/shard_map/while/body/eval_jaxpr/ppermute | solution.py:10
  85.2 16.1 %copy-start.3 = (s32[8]{0:T(128)S(1)}, s32[8]{0:T(128)}, u32[]{:S(2)}) copy-start(s32[8]{0:T(128)} %get-tuple-element.243) | copy-start | bytes 100 | tf_op jit(solution)/shard_map/while
  114.5 41.4 %collective-permute-start = (bf16[1536,256]{1,0:T(8,128)(2,1)S(1)}, bf16[1536,256]{1,0:T(8,128)(2,1)}, u32[]{:S(2)}, u32[]{:S(2)}) collective-permute-start(bf16[1536,256]{1,0:T(8,128)(2,1)S(1)} %copy.28), channel_id=1, source_target_pairs={{4,0},{8,4},{12,8},{16,12},{20,16},{24,20},{28,24},{32,28},{36,32}... | collective-permute-start | bytes 2359304 | tf_op jit(solution)/shard_map/while/body/eval_jaxpr/ppermute | solution.py:10
  127.2 16.1 %copy-start.3 = (s32[8]{0:T(128)S(1)}, s32[8]{0:T(128)}, u32[]{:S(2)}) copy-start(s32[8]{0:T(128)} %get-tuple-element.243) | copy-start | bytes 100 | tf_op jit(solution)/shard_map/while
  157.0 41.1 %collective-permute-start = (bf16[1536,256]{1,0:T(8,128)(2,1)S(1)}, bf16[1536,256]{1,0:T(8,128)(2,1)}, u32[]{:S(2)}, u32[]{:S(2)}) collective-permute-start(bf16[1536,256]{1,0:T(8,128)(2,1)S(1)} %copy.28), channel_id=1, source_target_pairs={{4,0},{8,4},{12,8},{16,12},{20,16},{24,20},{28,24},{32,28},{36,32}... | collective-permute-start | bytes 2359304 | tf_op jit(solution)/shard_map/while/body/eval_jaxpr/ppermute | solution.py:10
  169.4 16.1 %copy-start.3 = (s32[8]{0:T(128)S(1)}, s32[8]{0:T(128)}, u32[]{:S(2)}) copy-start(s32[8]{0:T(128)} %get-tuple-element.243) | copy-start | bytes 100 | tf_op jit(solution)/shard_map/while
  199.2 41.1 %collective-permute-start = (bf16[1536,256]{1,0:T(8,128)(2,1)S(1)}, bf16[1536,256]{1,0:T(8,128)(2,1)}, u32[]{:S(2)}, u32[]{:S(2)}) collective-permute-start(bf16[1536,256]{1,0:T(8,128)(2,1)S(1)} %copy.28), channel_id=1, source_target_pairs={{4,0},{8,4},{12,8},{16,12},{20,16},{24,20},{28,24},{32,28},{36,32}... | collective-permute-start | bytes 2359304 | tf_op jit(solution)/shard_map/while/body/eval_jaxpr/ppermute | solution.py:10
  211.7 16.1 %copy-start.3 = (s32[8]{0:T(128)S(1)}, s32[8]{0:T(128)}, u32[]{:S(2)}) copy-start(s32[8]{0:T(128)} %get-tuple-element.243) | copy-start | bytes 100 | tf_op jit(solution)/shard_map/while
  241.5 43.5 %collective-permute-start = (bf16[1536,256]{1,0:T(8,128)(2,1)S(1)}, bf16[1536,256]{1,0:T(8,128)(2,1)}, u32[]{:S(2)}, u32[]{:S(2)}) collective-permute-start(bf16[1536,256]{1,0:T(8,128)(2,1)S(1)} %copy.28), channel_id=1, source_target_pairs={{4,0},{8,4},{12,8},{16,12},{20,16},{24,20},{28,24},{32,28},{36,32}... | collective-permute-start | bytes 2359304 | tf_op jit(solution)/shard_map/while/body/eval_jaxpr/ppermute | solution.py:10
  256.3 16.1 %copy-start.3 = (s32[8]{0:T(128)S(1)}, s32[8]{0:T(128)}, u32[]{:S(2)}) copy-start(s32[8]{0:T(128)} %get-tuple-element.243) | copy-start | bytes 100 | tf_op jit(solution)/shard_map/while
  286.1 41.4 %collective-permute-start = (bf16[1536,256]{1,0:T(8,128)(2,1)S(1)}, bf16[1536,256]{1,0:T(8,128)(2,1)}, u32[]{:S(2)}, u32[]{:S(2)}) collective-permute-start(bf16[1536,256]{1,0:T(8,128)(2,1)S(1)} %copy.28), channel_id=1, source_target_pairs={{4,0},{8,4},{12,8},{16,12},{20,16},{24,20},{28,24},{32,28},{36,32}... | collective-permute-start | bytes 2359304 | tf_op jit(solution)/shard_map/while/body/eval_jaxpr/ppermute | solution.py:10
  298.8 16.1 %copy-start.3 = (s32[8]{0:T(128)S(1)}, s32[8]{0:T(128)}, u32[]{:S(2)}) copy-start(s32[8]{0:T(128)} %get-tuple-element.243) | copy-start | bytes 100 | tf_op jit(solution)/shard_map/while
  328.6 41.1 %collective-permute-start = (bf16[1536,256]{1,0:T(8,128)(2,1)S(1)}, bf16[1536,256]{1,0:T(8,128)(2,1)}, u32[]{:S(2)}, u32[]{:S(2)}) collective-permute-start(bf16[1536,256]{1,0:T(8,128)(2,1)S(1)} %copy.28), channel_id=1, source_target_pairs={{4,0},{8,4},{12,8},{16,12},{20,16},{24,20},{28,24},{32,28},{36,32}... | collective-permute-start | bytes 2359304 | tf_op jit(solution)/shard_map/while/body/eval_jaxpr/ppermute | solution.py:10
  341.1 16.1 %copy-start.3 = (s32[8]{0:T(128)S(1)}, s32[8]{0:T(128)}, u32[]{:S(2)}) copy-start(s32[8]{0:T(128)} %get-tuple-element.243) | copy-start | bytes 100 | tf_op jit(solution)/shard_map/while
  395.3 10.0 %copy-start.1 = (f32[1536,256]{1,0:T(8,128)S(1)}, f32[1536,256]{1,0:T(8,128)}, u32[]{:S(2)}) copy-start(f32[1536,256]{1,0:T(8,128)} %get-tuple-element.128) | copy-start | bytes 4718596
  403.5 3.3 copy-start.2
  406.7 191.2 %all-reduce.3.cloned.1.call-start = ((), (), s32[]{:S(2)}) async-start(), calls=%async_computation.2 | async-start | bytes 1048576 | tf_op jit(solution)/shard_map/psum | solution.py:98
Sparse Core Ops, SparseCore 0:
  406.9 38.6 reduce-scatter.1
  451.7 146.2 all-reduce.2
where the time goes:
time: 610 us; the launch traced here: 608 us
  waiting for transfers between devices  237 us (39%)
  local copies, waits for them, and re-layouts  177 us (29%)
  matrix products  139 us (23%)
  other arithmetic  29.8 us (5%)
  between operations  14.1 us (2%)
  starting transfers between devices  11.7 us (2%)
    psum x1, waiting for transfers between devices, on_device(): grad_self, grad_neigh = lax.psum((self_term, neigh_term), ('dom', 'rep'))  146 us
    while x35, local copies, waits for them, and re-layouts  132 us
    dot_general x8, matrix products, step_terms(): jnp.einsum('kij,kjf->kif', weights_now, picked, preferred_element_type=jn...  63.2 us
    dot_general x8, matrix products, step_terms(): jnp.dot(placing, product.reshape(slot_total, tile_side * width), precisio...  55 us
    ppermute x10, waiting for transfers between devices, passed_along(): return lax.ppermute(block, axis, route)  52.5 us
    reduce_scatter x1, waiting for transfers between devices, on_device(): lax.psum_scatter(partial_value, 'rep', scatter_dimension=0, tiled=True)  37.6 us
    add x7, other arithmetic, turn_one(): partial_value = partial_value + contribution(current, turn_index)  22.1 us
    unnamed x10, local copies, waits for them, and re-layouts  17.1 us
  transfers between devices with their start and end apart: 12, of which 5 were waited for; matrix products, arithmetic and copies ran while one was open for 48% of the time, Pallas kernels for 0%

commit v1 on v0

v1 whole, which is shorter than its diff:
```python
import functools

import jax
import jax.numpy as jnp
from jax import lax
from jax.experimental import pallas as pl
from jax.experimental.pallas import tpu as pltpu
from jax.sharding import PartitionSpec as P

MESH = pl.DeviceIdType.MESH
BLOCKS = 32
STEPS = 8
SLOTS = 88
TILE = 128
RT = 12
WIDTH = 256
SUBS = 3
SUB = 256
ROWS = 1536
QUARTER = 384


def where_am_i():
    p = lax.axis_index("dom")
    rep = lax.axis_index("rep")
    copy, core = rep // 2, rep % 2
    g = (p + 16 * copy) % BLOCKS
    return copy, core, g


def device(copy, g, core):
    return ((g + 16 * copy) % BLOCKS, 2 * copy + core)


def at(z, y):
    return (z % 8) * 4 + y


def aggregate_kernel(
    slots,
    features,
    weights,
    weight_self,
    weight_neigh,
    cotangent,
    out_ref,
    self_ref,
    neigh_ref,
    wbuf,
    fbuf,
    obuf,
    acc,
    r1buf,
    r1src,
    r2src,
    r2buf,
    w_sem,
    own_sem,
    f_sem,
    o_sem,
    r1_sem,
    r2_sem,
    s_swap,
    s_y,
    s_yr,
    s_zd,
    s_zu,
    s_rd,
    s_ru,
    s_x,
    s_x2,
    s_o,
    s_r1,
    s_r2,
):
    k, c, g = where_am_i()
    z, y = g // 4, g % 4
    first, mine_no = k, 1 - k

    here = device(k, g, c)
    other_core = device(k, g, 1 - c)
    other_copy = device(1 - k, g, c)
    y_up, y_down = (y + 1) % 4, (y + 3) % 4
    to_y_up = device(k, at(z, y_up), c)
    to_y_down = device(k, at(z, y_down), c)
    to_z_down = device(k, at(z + 7, y), c)
    to_z_up = device(k, at(z + 1, y), c)
    to_z_flip = device(k, at(z + 5, y), c)
    to_z_flip_back = device(k, at(z + 3, y), c)
    to_twin = device(k, (g + 16) % BLOCKS, c)
    to_rep = device(1 - k, (g + 16) % BLOCKS, c)
    del here

    for step in range(STEPS):
        pltpu.make_async_copy(
            weights.at[pl.ds(step * SLOTS, SLOTS)], wbuf.at[pl.ds(step * SLOTS, SLOTS)], w_sem.at[step]
        ).start()

    barrier = pltpu.get_barrier_semaphore()
    partners = (
        other_core,
        other_copy,
        to_y_up,
        to_y_down,
        to_z_down,
        to_z_up,
        to_z_flip,
        to_z_flip_back,
        to_twin,
        to_rep,
    )
    for partner in partners:
        pl.semaphore_signal(barrier, inc=1, device_id=partner, device_id_type=MESH)
    wbuf[STEPS * SLOTS] = jnp.zeros((TILE, TILE), wbuf.dtype)
    pl.semaphore_wait(barrier, len(partners))

    def push(slot_from, sub_from, slot_to, send_sem, target):
        pltpu.make_async_remote_copy(
            src_ref=fbuf.at[slot_from, sub_from],
            dst_ref=fbuf.at[slot_to, sub_from],
            send_sem=send_sem,
            recv_sem=f_sem.at[slot_to, sub_from],
            device_id=target,
            device_id_type=MESH,
        ).start()

    def arrived(slot, sub):
        pltpu.make_async_copy(fbuf.at[slot, sub], fbuf.at[slot, sub], f_sem.at[slot, sub]).wait()

    def sent(sem):
        pltpu.make_async_copy(fbuf.at[0, 0], fbuf.at[0, 0], sem).wait()

    def give_core(slot):
        half = slot // STEPS
        pltpu.make_async_remote_copy(
            src_ref=fbuf.at[slot],
            dst_ref=obuf.at[slot % STEPS],
            send_sem=s_o.at[slot % STEPS],
            recv_sem=o_sem.at[slot % STEPS],
            device_id=other_core,
            device_id_type=MESH,
        ).start()
        del half

    def swap(sub, target):
        pltpu.make_async_remote_copy(
            src_ref=features.at[c, sub],
            dst_ref=fbuf.at[4, sub],
            send_sem=s_swap.at[sub],
            recv_sem=f_sem.at[4, sub],
            device_id=target,
            device_id_type=MESH,
        ).start()

    sender = jnp.logical_or(jnp.logical_and(k == 0, c == 0), jnp.logical_and(k == 1, c == 1))

    @pl.when(jnp.logical_and(k == 0, c == 0))
    def _():
        for sub in range(SUBS):
            swap(sub, other_copy)

    @pl.when(jnp.logical_and(k == 1, c == 1))
    def _():
        for sub in range(SUBS):
            swap(sub, to_twin)

    @pl.when(k == 0)
    def _():
        for sub in range(SUBS):
            pltpu.make_async_copy(features.at[c, sub], fbuf.at[4, sub], f_sem.at[4, sub]).start()

    def z_sends(slot, block_y, j):
        delta = block_y - y
        for n, sub in enumerate((first, 2)):
            push(slot, sub, 8 + delta, s_zd.at[j, n], to_z_down)
        above = delta >= 0
        z_to = jnp.where(above, z + 1, z + 5)
        target = device(k, at(z_to, y), c)
        for n, sub in enumerate((first, 2)):
            push(slot, sub, (delta + 16) % 16, s_zu.at[j, n], target)

    for sub in range(SUBS):
        arrived(4, sub)
        push(4, sub, 4 + y - y_up, s_y.at[0, sub], to_y_up)
        push(4, sub, 4 + y - y_down, s_y.at[1, sub], to_y_down)
    z_sends(4, y, 0)

    @pl.when(c == 1)
    def _():
        give_core(4)

    from_up = 4 + y_up - y
    from_down = 4 + y_down - y
    for sub in range(SUBS):
        arrived(from_down, sub)
        if sub != 1:
            push(from_down, sub, 4 + y_down - y_up, s_yr.at[sub], to_y_up)
        arrived(from_up, sub)
        if sub == 1:
            push(from_up, sub, 4 + y_up - y_down, s_yr.at[sub], to_y_down)
    z_sends(from_up, y_up, 1)
    z_sends(from_down, y_down, 3)

    @pl.when(c == 1)
    def _():
        give_core(from_up)
        give_core(from_down)

    opposite = (y + 2) % 4
    from_opposite = 4 + opposite - y
    for sub in range(SUBS):
        arrived(from_opposite, sub)
    z_sends(from_opposite, opposite, 2)

    @pl.when(c == 1)
    def _():
        give_core(from_opposite)

    acc[...] = jnp.zeros_like(acc)
    for step in range(STEPS):
        pltpu.make_async_copy(
            weights.at[pl.ds(step * SLOTS, SLOTS)], wbuf.at[pl.ds(step * SLOTS, SLOTS)], w_sem.at[step]
        ).wait()

    group = 3

    def multiply(slot):
        step = slot % STEPS
        pltpu.make_async_copy(obuf.at[step], obuf.at[step], o_sem.at[step]).wait()
        half_cols = RT // 2

        def rows_of(r, carry):
            base = step * (RT * RT) + r * (group * RT)
            total = None
            for ref, at_slot, side in ((fbuf, slot, c), (obuf, step, 1 - c)):
                stacked = []
                for n in range(group):
                    tiles = [
                        wbuf[slots[base + n * RT + half_cols * side + i]] for i in range(half_cols)
                    ]
                    stacked.append(jnp.concatenate(tiles, axis=1))
                lhs = jnp.concatenate(stacked, axis=0)
                rhs = ref[at_slot].reshape(SUBS * SUB, WIDTH)
                term = jnp.dot(lhs, rhs, preferred_element_type=jnp.float32)
                total = term if total is None else total + term
            window = pl.ds(pl.multiple_of(r * (group * TILE), group * TILE), group * TILE)
            acc[window, :] += total
            return carry

        lax.fori_loop(0, RT // group, rows_of, 0)

    def order(i):
        return i + i // 2 - 2 * (i // 3)

    def delta_of(i):
        return (y + order(i)) % 4 - y

    def first_pass(i, carry):
        delta = delta_of(i)
        above = 8 + delta
        below = (delta + 16) % 16
        far = 12 + delta
        arrived(above, first)
        push(above, first, far, s_rd.at[i], to_z_down)
        push(above, first, above, s_x.at[0, i], other_copy)
        arrived(above, 2)
        arrived(below, first)
        push(below, first, below, s_x.at[1, i], other_copy)
        arrived(below, 2)
        z_to = jnp.where(delta >= 0, z + 5, z + 1)
        push(below, 2, far, s_ru.at[i], device(k, at(z_to, y), c))

        @pl.when(c == 0)
        def _():
            multiply(4 + delta)

        return carry

    lax.fori_loop(0, 4, first_pass, 0)

    def second_pass(i, carry):
        delta = delta_of(i)
        above = 8 + delta
        below = (delta + 16) % 16
        far = 12 + delta
        arrived(far, first)
        push(far, first, far, s_x2.at[i], other_copy)
        arrived(above, mine_no)
        arrived(below, mine_no)
        mine = jnp.where(above // STEPS == c, above, below)
        theirs = above + below - mine
        give_core(theirs)
        multiply(mine)
        return carry

    lax.fori_loop(0, 4, second_pass, 0)

    def third_pass(i, carry):
        far = 12 + delta_of(i)
        arrived(far, 2)
        arrived(far, mine_no)

        @pl.when(c == 0)
        def _():
            give_core(far)

        @pl.when(c == 1)
        def _():
            multiply(far)

        return carry

    lax.fori_loop(0, 4, third_pass, 0)

    for part in range(2):
        start = pl.multiple_of((2 * part + 1 - c) * QUARTER, QUARTER)
        r1src[part] = acc[pl.ds(start, QUARTER), :]
        pltpu.make_async_remote_copy(
            src_ref=r1src.at[part],
            dst_ref=r1buf.at[part],
            send_sem=s_r1.at[part],
            recv_sem=r1_sem.at[part],
            device_id=other_core,
            device_id_type=MESH,
        ).start()

    for sem in [s_y.at[d, s] for d in range(2) for s in range(SUBS)] + [s_yr.at[s] for s in range(SUBS)]:
        sent(sem)
    for j in range(4):
        for n in range(2):
            sent(s_zd.at[j, n])
            sent(s_zu.at[j, n])
            sent(s_x.at[n, j])
        sent(s_rd.at[j])
        sent(s_ru.at[j])
        sent(s_x2.at[j])
    for step in range(STEPS):
        pltpu.make_async_copy(obuf.at[step], obuf.at[step], s_o.at[step]).wait()

    @pl.when(sender)
    def _():
        for sub in range(SUBS):
            sent(s_swap.at[sub])

    for part in range(2):
        pltpu.make_async_copy(r1buf.at[part], r1buf.at[part], r1_sem.at[part]).wait()

    away = pl.multiple_of((2 * (1 - k) + c) * QUARTER, QUARTER)
    r2src[...] = (acc[pl.ds(away, QUARTER), :] + r1buf[1 - k]).astype(r2src.dtype)
    cross = pltpu.make_async_remote_copy(
        src_ref=r2src,
        dst_ref=r2buf,
        send_sem=s_r2,
        recv_sem=r2_sem,
        device_id=to_rep,
        device_id_type=MESH,
    )
    cross.start()
    home = pl.multiple_of((2 * k + c) * QUARTER, QUARTER)
    kept = acc[pl.ds(home, QUARTER), :] + r1buf[k]
    own = features.reshape(ROWS, WIDTH)[pl.ds(home, QUARTER), :]
    pre = jnp.dot(own, weight_self[...], preferred_element_type=jnp.float32)
    cross.wait()
    aggregate = (kept + r2buf[...].astype(jnp.float32)).astype(jnp.bfloat16)
    pre = pre + jnp.dot(aggregate, weight_neigh[...], preferred_element_type=jnp.float32)
    sigmoid = jax.nn.sigmoid(pre)
    out_ref[...] = (pre * sigmoid).astype(out_ref.dtype)
    slope = (cotangent[...].astype(jnp.float32) * sigmoid * (1.0 + pre * (1.0 - sigmoid))).astype(
        jnp.bfloat16
    )
    contract = (((0,), (0,)), ((), ()))
    self_ref[...] = lax.dot_general(own, slope, contract, preferred_element_type=jnp.float32)
    neigh_ref[...] = lax.dot_general(aggregate, slope, contract, preferred_element_type=jnp.float32)
    for part in range(2):
        pltpu.make_async_copy(r1src.at[part], r1src.at[part], s_r1.at[part]).wait()


def slot_table(rows, cols, counts):
    steps, slots = rows.shape
    key = rows * RT + cols
    live = jnp.arange(slots, dtype=jnp.int32)[None, :] < counts[:, None]
    number = jnp.arange(steps * slots, dtype=jnp.int32).reshape(steps, slots)
    hit = (key[:, None, :] == jnp.arange(RT * RT, dtype=jnp.int32)[None, :, None]) & live[:, None, :]
    found = jnp.max(jnp.where(hit, number[:, None, :], -1), axis=2)
    return jnp.where(found < 0, steps * slots, found).reshape(-1)


def on_device(
    features, tile_weights, tile_rows, tile_cols, tile_counts, weight_self, weight_neigh, cotangent
):
    table = slot_table(tile_rows[0, 0], tile_cols[0, 0], tile_counts[0, 0])
    weights = tile_weights.reshape(STEPS * SLOTS, TILE, TILE)
    vmem = pl.BlockSpec(memory_space=pltpu.VMEM)
    dma = pltpu.SemaphoreType.DMA
    output, self_term, neigh_term = pl.pallas_call(
        aggregate_kernel,
        out_shape=(
            jax.ShapeDtypeStruct((QUARTER, WIDTH), jnp.bfloat16),
            jax.ShapeDtypeStruct((WIDTH, WIDTH), jnp.float32),
            jax.ShapeDtypeStruct((WIDTH, WIDTH), jnp.float32),
        ),
        in_specs=[
            pl.BlockSpec(memory_space=pltpu.SMEM),
            vmem,
            pl.BlockSpec(memory_space=pl.ANY),
            vmem,
            vmem,
            vmem,
        ],
        out_specs=(vmem, vmem, vmem),
        scratch_shapes=[
            pltpu.VMEM((STEPS * SLOTS + 1, TILE, TILE), jnp.bfloat16),
            pltpu.VMEM((2 * STEPS, SUBS, SUB, WIDTH), jnp.bfloat16),
            pltpu.VMEM((STEPS, SUBS, SUB, WIDTH), jnp.bfloat16),
            pltpu.VMEM((ROWS, WIDTH), jnp.float32),
            pltpu.VMEM((2, QUARTER, WIDTH), jnp.float32),
            pltpu.VMEM((2, QUARTER, WIDTH), jnp.float32),
            pltpu.VMEM((QUARTER, WIDTH), jnp.bfloat16),
            pltpu.VMEM((QUARTER, WIDTH), jnp.bfloat16),
            dma((STEPS,)),
            dma((1,)),
            dma((2 * STEPS, SUBS)),
            dma((STEPS,)),
            dma((2,)),
            dma,
            dma((SUBS,)),
            dma((2, SUBS)),
            dma((SUBS,)),
            dma((4, 2)),
            dma((4, 2)),
            dma((4,)),
            dma((4,)),
            dma((2, 4)),
            dma((4,)),
            dma((STEPS,)),
            dma((2,)),
            dma,
        ],
        compiler_params=pltpu.CompilerParams(
            collective_id=0, has_side_effects=True, vmem_limit_bytes=60 * 1024 * 1024
        ),
    )(
        table,
        features.reshape(2, SUBS, SUB, WIDTH),
        weights,
        weight_self,
        weight_neigh,
        cotangent,
    )
    grad_self, grad_neigh = lax.psum((self_term, neigh_term), ("dom", "rep"))
    return (output, grad_self, grad_neigh)


def solution(mesh):
    return jax.shard_map(
        on_device,
        mesh=mesh,
        in_specs=(
            P("dom", None),
            P("dom", "rep", None, None, None, None),
            P("dom", "rep", None, None),
            P("dom", "rep", None, None),
            P("dom", "rep", None),
            P(),
            P(),
            P(("dom", "rep"), None),
        ),
        out_specs=(P(("dom", "rep"), None), P(), P()),
        check_vma=False,
    )
```

time: 610 us -> 262 us (0.43)
  local copies, waits for them, and re-layouts: 177 us -> 5.03 us
  matrix products: 139 us -> 0 us
  Pallas kernels: 0 us -> 76 us
  waiting for transfers between devices: 237 us -> 164 us
  other arithmetic: 29.8 us -> 2.41 us
  starting transfers between devices: 11.7 us -> 0.04 us
    dot_general x28 -> x0, matrix products: 139 us -> none  [the longest x8 63.2 us: step_terms(): jnp.einsum('kij,kjf->kif', weights_now, picked, preferred_element_type=jn...]
    while x35 -> x0, local copies, waits for them, and re-layouts: 132 us -> none
    pallas_call x0 -> x1, Pallas kernels: none -> 76 us  [on_device(): pl.pallas_call(aggregate_kernel, out_shape=(jax.ShapeDtypeStruct((QUARTER...]
    ppermute x10 -> x0, waiting for transfers between devices: 52.5 us -> none  [passed_along(): return lax.ppermute(block, axis, route)]
    reduce_scatter x1 -> x0, waiting for transfers between devices: 37.6 us -> none  [on_device(): lax.psum_scatter(partial_value, 'rep', scatter_dimension=0, tiled=True)]
    add x8 -> x1, other arithmetic: 23.5 us -> 0.71 us  [slot_table(): key = rows * RT + cols]
    psum x1, waiting for transfers between devices: 146 us -> 164 us  [on_device(): grad_self, grad_neigh = lax.psum((self_term, neigh_term), ('dom', 'rep'))]
    reshape x16 -> x0, local copies, waits for them, and re-layouts: 16.5 us -> none  [the longest x8 11.3 us: step_terms(): return summed.reshape(feature_block.shape[0], width)]
  transfers between devices with their start and end apart: 12 -> 1, of which waited for: 5 -> 1; matrix products, arithmetic and copies ran while one was open for 48% -> 0% of each run, Pallas kernels for 0% -> 0%
where the time goes in v1:
time: 262 us
  waiting for transfers between devices  164 us (63%)
  Pallas kernels  76 us (29%)
  between operations  14.1 us (5%)
  local copies, waits for them, and re-layouts  5.03 us (2%)
    psum x1, waiting for transfers between devices, on_device(): grad_self, grad_neigh = lax.psum((self_term, neigh_term), ('dom', 'rep'))  164 us
    pallas_call x1, Pallas kernels, on_device(): pl.pallas_call(aggregate_kernel, out_shape=(jax.ShapeDtypeStruct((QUARTER...  76 us
  transfers between devices with their start and end apart: 1, of which 1 were waited for; matrix products, arithmetic and copies ran while one was open for 0% of the time, Pallas kernels for 0%

profile of v1, /device:TPU:1, one launch (start us, length us, event | category | flops | bytes accessed | tf_op | source)
XLA Modules:
  0.0 261.8 jit_solution(7294081640551831479)
XLA Ops:
  7.2 0.0 all-reduce.3.cloned.1.call-start
  7.2 0.7 iota_compare_fusion.1
  8.0 0.7 add_bitcast_fusion
  8.7 0.4 select_reduce_fusion
  9.0 0.1 reduce_max.12
  9.1 0.6 compare_select_fusion.slots
  9.7 76.0 %shard_map.103 = (bf16[384,256]{1,0:T(8,128)(2,1)}, f32[256,256]{1,0:T(8,128)}, f32[256,256]{1,0:T(8,128)}) custom-call(s32[1152]{0:T(1024)} %compare_select_fusion.slots, bf16[2,3,256,256]{3,2,1,0:T(8,128)(2,1)} %bitcast.6, bf16[704,128,128]{2,1,0:T(8,128)(2,1)} %bitcast.5, bf16[256,256]{1,0:T(8,128)(2,1)} %weight_self.1, bf16[256,256]{1,0:T(8,128)(2,1)} %weight_neigh.1, ...), custom_call_target="tpu_custom_call" | custom-call | tf_op jit(solution)/shard_map/pallas_call | solution.py:395
  85.7 0.0 all-reduce.3.cloned.1.call-update
  85.7 164.3 %all-reduce.3.cloned.1.call-done = (f32[256,256]{1,0:T(8,128)}, f32[256,256]{1,0:T(8,128)}) async-done(((f32[256,256]{1,0:T(8,128)}, f32[256,256]{1,0:T(8,128)}), (f32[256,256]{1,0:T(8,128)}, f32[256,256]{1,0:T(8,128)})) %all-reduce.3.cloned.1.call-update) | async-done | bytes 524304 | tf_op jit(solution)/shard_map/psum | solution.py:450
  250.0 1.6 copy.16
  251.6 1.7 copy.17
  253.3 1.7 copy.18
  (1 shorter events, 0.0 us)
Async XLA Ops:
  7.2 242.8 %all-reduce.3.cloned.1.call-start = ((), (), s32[]{:S(2)}) async-start(), calls=%async_computation | async-start | bytes 1048576 | tf_op jit(solution)/shard_map/psum | solution.py:450
Sparse Core Ops, SparseCore 0:
  85.8 164.1 all-reduce.2

commit v2 on v1

--- a/solution.py
+++ b/solution.py
@@ -1,5 +1,3 @@
-import functools
-
 import jax
 import jax.numpy as jnp
 from jax import lax
@@ -18,6 +16,7 @@
 SUB = 256
 ROWS = 1536
 QUARTER = 384
+CHIPS = 64
 
 
 def where_am_i():
@@ -72,12 +71,25 @@
     s_o,
     s_r1,
     s_r2,
+    gsrc,
+    gin,
+    gsum,
+    rsbuf,
+    agbuf,
+    agother,
+    g0_sem,
+    rs_sem,
+    ag_sem,
+    g1_sem,
+    s_g0,
+    s_rs,
+    s_ag,
+    s_g1,
 ):
     k, c, g = where_am_i()
     z, y = g // 4, g % 4
     first, mine_no = k, 1 - k
 
-    here = device(k, g, c)
     other_core = device(k, g, 1 - c)
     other_copy = device(1 - k, g, c)
     y_up, y_down = (y + 1) % 4, (y + 3) % 4
@@ -89,7 +101,6 @@
     to_z_flip_back = device(k, at(z + 3, y), c)
     to_twin = device(k, (g + 16) % BLOCKS, c)
     to_rep = device(1 - k, (g + 16) % BLOCKS, c)
-    del here
 
     for step in range(STEPS):
         pltpu.make_async_copy(
@@ -131,7 +142,6 @@
         pltpu.make_async_copy(fbuf.at[0, 0], fbuf.at[0, 0], sem).wait()
 
     def give_core(slot):
-        half = slot // STEPS
         pltpu.make_async_remote_copy(
             src_ref=fbuf.at[slot],
             dst_ref=obuf.at[slot % STEPS],
@@ -140,7 +150,6 @@
             device_id=other_core,
             device_id_type=MESH,
         ).start()
-        del half
 
     def swap(sub, target):
         pltpu.make_async_remote_copy(
@@ -369,10 +378,76 @@
         jnp.bfloat16
     )
     contract = (((0,), (0,)), ((), ()))
-    self_ref[...] = lax.dot_general(own, slope, contract, preferred_element_type=jnp.float32)
-    neigh_ref[...] = lax.dot_general(aggregate, slope, contract, preferred_element_type=jnp.float32)
+    self_term = lax.dot_general(own, slope, contract, preferred_element_type=jnp.float32)
+    neigh_term = lax.dot_general(aggregate, slope, contract, preferred_element_type=jnp.float32)
+    gsrc[...] = jnp.where(c == 0, neigh_term, self_term)
+    core_swap = pltpu.make_async_remote_copy(
+        src_ref=gsrc,
+        dst_ref=gin,
+        send_sem=s_g0,
+        recv_sem=g0_sem,
+        device_id=other_core,
+        device_id_type=MESH,
+    )
+    core_swap.start()
     for part in range(2):
         pltpu.make_async_copy(r1src.at[part], r1src.at[part], s_r1.at[part]).wait()
+    core_swap.wait()
+    chip_term = jnp.where(c == 0, self_term, neigh_term) + gin[...]
+    for side in range(2):
+        gsum[:, side] = chip_term[:, side * TILE : (side + 1) * TILE].reshape(CHIPS // 2, 8, TILE)
+    me = 32 * k + g
+
+    def scatter(t, carry):
+        peer = (me + t) % CHIPS
+        pltpu.make_async_remote_copy(
+            src_ref=gsum.at[peer // 2, peer % 2],
+            dst_ref=rsbuf.at[t - 1],
+            send_sem=s_rs,
+            recv_sem=rs_sem,
+            device_id=device(peer // 32, peer % 32, c),
+            device_id_type=MESH,
+        ).start()
+        return carry
+
+    lax.fori_loop(1, CHIPS, scatter, 0)
+    everything = pltpu.make_async_copy(rsbuf, rsbuf, rs_sem)
+    everything.wait()
+    piece = gsum[me // 2, me % 2] + jnp.sum(rsbuf[...], axis=0)
+    agbuf[me // 2, me % 2] = piece
+
+    def gather(t, carry):
+        peer = (me + t) % CHIPS
+        pltpu.make_async_remote_copy(
+            src_ref=agbuf.at[me // 2, me % 2],
+            dst_ref=agbuf.at[me // 2, me % 2],
+            send_sem=s_ag,
+            recv_sem=ag_sem,
+            device_id=device(peer // 32, peer % 32, c),
+            device_id_type=MESH,
+        ).start()
+        return carry
+
+    lax.fori_loop(1, CHIPS, gather, 0)
+    pltpu.make_async_copy(rsbuf, rsbuf, s_rs).wait()
+    pltpu.make_async_copy(rsbuf, rsbuf, ag_sem).wait()
+    last = pltpu.make_async_remote_copy(
+        src_ref=agbuf,
+        dst_ref=agother,
+        send_sem=s_g1,
+        recv_sem=g1_sem,
+        device_id=other_core,
+        device_id_type=MESH,
+    )
+    last.start()
+    pltpu.make_async_copy(rsbuf, rsbuf, s_ag).wait()
+    last.wait()
+    for side in range(2):
+        lanes = slice(side * TILE, (side + 1) * TILE)
+        held = agbuf[:, side].reshape(WIDTH, TILE)
+        came = agother[:, side].reshape(WIDTH, TILE)
+        self_ref[:, lanes] = jnp.where(c == 0, held, came)
+        neigh_ref[:, lanes] = jnp.where(c == 0, came, held)
 
 
 def slot_table(rows, cols, counts):
@@ -392,7 +467,7 @@
     weights = tile_weights.reshape(STEPS * SLOTS, TILE, TILE)
     vmem = pl.BlockSpec(memory_space=pltpu.VMEM)
     dma = pltpu.SemaphoreType.DMA
-    output, self_term, neigh_term = pl.pallas_call(
+    return pl.pallas_call(
         aggregate_kernel,
         out_shape=(
             jax.ShapeDtypeStruct((QUARTER, WIDTH), jnp.bfloat16),
@@ -435,6 +510,20 @@
             dma((STEPS,)),
             dma((2,)),
             dma,
+            pltpu.VMEM((WIDTH, WIDTH), jnp.float32),
+            pltpu.VMEM((WIDTH, WIDTH), jnp.float32),
+            pltpu.VMEM((CHIPS // 2, 2, 8, TILE), jnp.float32),
+            pltpu.VMEM((CHIPS - 1, 8, TILE), jnp.float32),
+            pltpu.VMEM((CHIPS // 2, 2, 8, TILE), jnp.float32),
+            pltpu.VMEM((CHIPS // 2, 2, 8, TILE), jnp.float32),
+            dma,
+            dma,
+            dma,
+            dma,
+            dma,
+            dma,
+            dma,
+            dma,
         ],
         compiler_params=pltpu.CompilerParams(
             collective_id=0, has_side_effects=True, vmem_limit_bytes=60 * 1024 * 1024
@@ -447,8 +536,6 @@
         weight_neigh,
         cotangent,
     )
-    grad_self, grad_neigh = lax.psum((self_term, neigh_term), ("dom", "rep"))
-    return (output, grad_self, grad_neigh)
 
 
 def solution(mesh):

time: 262 us -> 122 us (0.47)
  waiting for transfers between devices: 164 us -> 0 us
  Pallas kernels: 76 us -> 114 us
  between operations: 14.1 us -> 0.65 us
    psum x1 -> x0, waiting for transfers between devices: 164 us -> none  [on_device(): grad_self, grad_neigh = lax.psum((self_term, neigh_term), ('dom', 'rep'))]
    pallas_call x1, Pallas kernels: 76 us -> 114 us  [on_device(): pl.pallas_call(aggregate_kernel, out_shape=(jax.ShapeDtypeStruct((QUARTER...]
  transfers between devices with their start and end apart: 1 -> 0, of which waited for: 1 -> 0; matrix products, arithmetic and copies ran while one was open for 0% -> 0% of each run, Pallas kernels for 0% -> 0%
where the time goes in v2:
time: 122 us
  Pallas kernels  114 us (93%)
  local copies, waits for them, and re-layouts  5.03 us (4%)
  other arithmetic  2.41 us (2%)
    pallas_call x1, Pallas kernels, on_device(): pl.pallas_call(aggregate_kernel, out_shape=(jax.ShapeDtypeStruct((QUARTER...  114 us
    unnamed x3, local copies, waits for them, and re-layouts  4.95 us

profile of v2, /device:TPU:1, one launch (start us, length us, event | category | flops | bytes accessed | tf_op | source)
XLA Modules:
  0.0 121.6 jit_solution(578794369447948871)
XLA Ops:
  0.6 0.7 iota_compare_fusion.1
  1.4 0.7 add_bitcast_fusion
  2.1 0.4 select_reduce_fusion
  2.4 0.1 reduce_max.12
  2.5 0.6 compare_select_fusion.slots
  3.1 113.5 %shard_map.103 = (bf16[384,256]{1,0:T(8,128)(2,1)}, f32[256,256]{1,0:T(8,128)}, f32[256,256]{1,0:T(8,128)}) custom-call(s32[1152]{0:T(1024)} %compare_select_fusion.slots, bf16[2,3,256,256]{3,2,1,0:T(8,128)(2,1)} %bitcast.6, bf16[704,128,128]{2,1,0:T(8,128)(2,1)} %bitcast.5, bf16[256,256]{1,0:T(8,128)(2,1)} %weight_self.1, bf16[256,256]{1,0:T(8,128)(2,1)} %weight_neigh.1, ...), custom_call_target="tpu_custom_call" | custom-call | tf_op jit(solution)/shard_map/pallas_call | solution.py:470
  116.7 1.6 %copy.14 = bf16[384,256]{1,0:T(8,128)(2,1)} copy(bf16[384,256]{1,0:T(8,128)(2,1)} %get-tuple-element.6) | data formatting | bytes 393216
  118.3 1.7 %copy.15 = f32[256,256]{1,0:T(8,128)} copy(f32[256,256]{1,0:T(8,128)} %get-tuple-element.7) | data formatting | bytes 524288
  119.9 1.7 %copy.16 = f32[256,256]{1,0:T(8,128)} copy(f32[256,256]{1,0:T(8,128)} %get-tuple-element.8) | data formatting | bytes 524288
  (1 shorter events, 0.0 us)

commit v3 on v2

v3 whole, which is shorter than its diff:
```python
import jax
import jax.numpy as jnp
from jax import lax
from jax.experimental import pallas as pl
from jax.experimental.pallas import tpu as pltpu
from jax.sharding import PartitionSpec as P

MESH = pl.DeviceIdType.MESH
BLOCKS = 32
STEPS = 8
SLOTS = 88
TILE = 128
RT = 12
WIDTH = 256
EDGE = 192
COMMON = 384
HALF = 768
ROWS = 1536
QUARTER = 384
CHIPS = 64


def where_am_i():
    p = lax.axis_index("dom")
    rep = lax.axis_index("rep")
    copy, core = rep // 2, rep % 2
    g = (p + 16 * copy) % BLOCKS
    return copy, core, g


def device(copy, g, core):
    return ((g + 16 * copy) % BLOCKS, 2 * copy + core)


def at(z, y):
    return (z % 8) * 4 + y


def aggregate_kernel(
    slots,
    features,
    weights,
    weight_self,
    weight_neigh,
    cotangent,
    out_ref,
    self_ref,
    neigh_ref,
    wbuf,
    fbuf,
    obuf,
    acc,
    r1buf,
    r2src,
    r2buf,
    w_sem,
    own_sem,
    f_sem,
    o_sem,
    r1_sem,
    r2_sem,
    s_swap,
    s_y,
    s_yr,
    s_zd,
    s_zu,
    s_rd,
    s_ru,
    s_x,
    s_x2,
    s_o,
    s_r1,
    s_r2,
    gsrc,
    gin,
    gsum,
    rsbuf,
    agbuf,
    agother,
    g0_sem,
    rs_sem,
    ag_sem,
    g1_sem,
    s_g0,
    s_rs,
    s_ag,
    s_g1,
    tbuf,
    t_sem,
    s_t,
    s_fy,
    s_fyr,
):
    k, c, g = where_am_i()
    z, y = g // 4, g % 4
    first, mine_no = k, 1 - k

    other_core = device(k, g, 1 - c)
    other_copy = device(1 - k, g, c)
    y_up, y_down = (y + 1) % 4, (y + 3) % 4
    to_y_up = device(k, at(z, y_up), c)
    to_y_down = device(k, at(z, y_down), c)
    to_z_down = device(k, at(z + 7, y), c)
    to_z_up = device(k, at(z + 1, y), c)
    to_z_flip = device(k, at(z + 5, y), c)
    to_z_flip_back = device(k, at(z + 3, y), c)
    to_twin = device(k, (g + 16) % BLOCKS, c)
    to_rep = device(1 - k, (g + 16) % BLOCKS, c)

    for step in range(STEPS):
        pltpu.make_async_copy(
            weights.at[pl.ds(step * SLOTS, SLOTS)], wbuf.at[pl.ds(step * SLOTS, SLOTS)], w_sem.at[step]
        ).start()

    barrier = pltpu.get_barrier_semaphore()
    partners = (
        other_core,
        other_copy,
        to_y_up,
        to_y_down,
        to_z_down,
        to_z_up,
        to_z_flip,
        to_z_flip_back,
        to_twin,
        to_rep,
    )
    for partner in partners:
        pl.semaphore_signal(barrier, inc=1, device_id=partner, device_id_type=MESH)
    wbuf[STEPS * SLOTS] = jnp.zeros((TILE, TILE), wbuf.dtype)
    pl.semaphore_wait(barrier, len(partners))

    subs = ((first, EDGE * k, EDGE), (2, 2 * EDGE, COMMON), (mine_no, EDGE * (1 - k), EDGE))

    def part_of(ref, n):
        _, start, size = subs[n]
        return ref.at[pl.ds(pl.multiple_of(start, EDGE), size)]

    def push(slot_from, n, slot_to, send_sem, target):
        pltpu.make_async_remote_copy(
            src_ref=part_of(fbuf.at[slot_from], n),
            dst_ref=part_of(fbuf.at[slot_to], n),
            send_sem=send_sem,
            recv_sem=f_sem.at[slot_to, subs[n][0]],
            device_id=target,
            device_id_type=MESH,
        ).start()

    def arrived(slot, n):
        here = part_of(fbuf.at[slot], n)
        pltpu.make_async_copy(here, here, f_sem.at[slot, subs[n][0]]).wait()

    def sent(sem, n):
        here = part_of(fbuf.at[0], n)
        pltpu.make_async_copy(here, here, sem).wait()

    def give_core(slot):
        pltpu.make_async_remote_copy(
            src_ref=fbuf.at[slot],
            dst_ref=obuf.at[slot % STEPS],
            send_sem=s_o.at[slot % STEPS],
            recv_sem=o_sem.at[slot % STEPS],
            device_id=other_core,
            device_id_type=MESH,
        ).start()

    cuts = ((0, 0, EDGE), (1, EDGE, EDGE), (2, 2 * EDGE, COMMON))

    def swap(target):
        for number, start, size in cuts:
            pltpu.make_async_remote_copy(
                src_ref=features.at[c, pl.ds(start, size)],
                dst_ref=fbuf.at[4, pl.ds(start, size)],
                send_sem=s_swap.at[number],
                recv_sem=f_sem.at[4, number],
                device_id=target,
                device_id_type=MESH,
            ).start()

    sender = jnp.logical_or(jnp.logical_and(k == 0, c == 0), jnp.logical_and(k == 1, c == 1))

    @pl.when(jnp.logical_and(k == 0, c == 0))
    def _():
        swap(other_copy)

    @pl.when(jnp.logical_and(k == 1, c == 1))
    def _():
        swap(to_twin)

    @pl.when(k == 0)
    def _():
        for number, start, size in cuts:
            pltpu.make_async_copy(
                features.at[c, pl.ds(start, size)], fbuf.at[4, pl.ds(start, size)], f_sem.at[4, number]
            ).start()

    edge_low = z % 4 == 0
    edge_high = z % 4 == 3
    to_plane = device(k, at(z + 3, y), c)

    def turns(edge, delta, j, n):
        if n == 0:
            return jnp.logical_and(edge, j != 0)
        return jnp.logical_and(edge, delta < 0)

    def z_sends(slot, block_y, j, n):
        delta = block_y - y
        turn = turns(edge_low, delta, j, n)

        @pl.when(turn)
        def _():
            pltpu.make_async_remote_copy(
                src_ref=part_of(fbuf.at[slot], n),
                dst_ref=part_of(tbuf.at[j], n),
                send_sem=s_zd.at[j, n],
                recv_sem=t_sem.at[j, n],
                device_id=to_plane,
                device_id_type=MESH,
            ).start()

        @pl.when(jnp.logical_not(turn))
        def _():
            push(slot, n, 8 + delta, s_zd.at[j, n], to_z_down)

        z_to = jnp.where(delta >= 0, z + 1, z + 5)
        target = device(k, at(z_to, y), c)
        push(slot, n, (delta + 16) % 16, s_zu.at[j, n], target)

    def turn_corner(delta, j, n):
        @pl.when(turns(edge_high, delta, j, n))
        def _():
            here = part_of(tbuf.at[j], n)
            pltpu.make_async_copy(here, here, t_sem.at[j, n]).wait()
            pltpu.make_async_remote_copy(
                src_ref=here,
                dst_ref=part_of(fbuf.at[8 + delta], n),
                send_sem=s_t.at[j, n],
                recv_sem=f_sem.at[8 + delta, subs[n][0]],
                device_id=to_twin,
                device_id_type=MESH,
            ).start()

    def share(slot, sem):
        push(slot, 0, slot, sem, other_copy)

    def share_edge(delta, i):
        above = 8 + delta
        below = (delta + 16) % 16
        arrived(below, 0)
        share(below, s_x.at[1, i])
        arrived(above, 0)
        share(above, s_x.at[0, i])

    for n in range(3):
        arrived(4, n)
        push(4, n, 4 + y - y_up, s_y.at[0, n], to_y_up)
        push(4, n, 4 + y - y_down, s_y.at[1, n], to_y_down)
        if n < 2:
            z_sends(4, y, 0, n)

    @pl.when(c == 1)
    def _():
        give_core(4)

    from_up = 4 + y_up - y
    from_down = 4 + y_down - y
    for n in range(3):
        if n == 0:
            arrived(8, 0)
            push(8, 0, 12, s_rd, to_z_down)
        if n == 1:
            arrived(0, 1)
            push(0, 1, 12, s_ru, device(k, at(z + 5, y), c))
        arrived(from_down, n)
        if n != 1:
            push(from_down, n, 4 + y_down - y_up, s_yr.at[n], to_y_up)
        if n == 0:
            z_sends(from_down, y_down, 3, n)
        arrived(from_up, n)
        if n == 1:
            push(from_up, n, 4 + y_up - y_down, s_yr.at[n], to_y_down)
        if n == 0:
            z_sends(from_up, y_up, 1, n)
        if n == 0:
            share(8, s_x.at[0, 0])
            arrived(0, 0)
            share(0, s_x.at[1, 0])

    @pl.when(c == 1)
    def _():
        give_core(from_up)
        give_core(from_down)

    opposite = (y + 2) % 4
    from_opposite = 4 + opposite - y
    arrived(from_opposite, 0)
    z_sends(from_opposite, opposite, 2, 0)
    z_sends(from_down, y_down, 3, 1)
    z_sends(from_up, y_up, 1, 1)
    arrived(from_opposite, 1)
    z_sends(from_opposite, opposite, 2, 1)
    arrived(from_opposite, 2)

    @pl.when(c == 1)
    def _():
        give_core(from_opposite)

    far_up = 12 + y_up - y
    far_down = 12 + y_down - y
    far_opposite = 12 + opposite - y

    def far_spread(n):
        arrived(12, n)
        push(12, n, 12 + y - y_up, s_fy.at[0, n], to_y_up)
        push(12, n, 12 + y - y_down, s_fy.at[1, n], to_y_down)

    far_spread(0)
    share(12, s_x2.at[0])
    turn_corner(y_up - y, 1, 0)
    turn_corner(y_down - y, 3, 0)
    share_edge(y_up - y, 1)
    share_edge(y_down - y, 3)

    acc[...] = jnp.zeros_like(acc)
    for step in range(STEPS):
        pltpu.make_async_copy(
            weights.at[pl.ds(step * SLOTS, SLOTS)], wbuf.at[pl.ds(step * SLOTS, SLOTS)], w_sem.at[step]
        ).wait()

    group = 6

    def multiply(slot):
        step = slot % STEPS
        pltpu.make_async_copy(obuf.at[step], obuf.at[step], o_sem.at[step]).wait()
        half_cols = RT // 2

        def rows_of(r, carry):
            base = step * (RT * RT) + r * (group * RT)
            total = None
            for ref, at_slot, side in ((fbuf, slot, c), (obuf, step, 1 - c)):
                stacked = []
                for n in range(group):
                    tiles = [
                        wbuf[slots[base + n * RT + half_cols * side + i]] for i in range(half_cols)
                    ]
                    stacked.append(jnp.concatenate(tiles, axis=1))
                lhs = jnp.concatenate(stacked, axis=0)
                term = jnp.dot(lhs, ref[at_slot], preferred_element_type=jnp.float32)
                total = term if total is None else total + term
            window = pl.ds(pl.multiple_of(r * (group * TILE), group * TILE), group * TILE)
            acc[window, :] += total
            return carry

        lax.fori_loop(0, RT // group, rows_of, 0)

    def order(i):
        return i + i // 2 - 2 * (i // 3)

    def delta_of(i):
        return (y + order(i)) % 4 - y

    def early_pass(i, carry):
        multiply(4 + delta_of(i))
        return carry

    def far_pass(i, carry):
        far = 12 + delta_of(i)
        arrived(far, 2)

        @pl.when(c == 0)
        def _():
            give_core(far)

        @pl.when(c == 1)
        def _():
            multiply(far)

        return carry

    def late_pass(i, carry):
        delta = delta_of(i)
        above = 8 + delta
        below = (delta + 16) % 16

        @pl.when(i > 0)
        def _():
            arrived(below, 1)

        arrived(above, 1)
        arrived(above, 2)
        arrived(below, 2)
        mine = jnp.where(above // STEPS == c, above, below)
        theirs = above + below - mine
        give_core(theirs)
        multiply(mine)
        return carry

    far_spread(1)
    arrived(far_down, 0)
    push(far_down, 0, 12 + y_down - y_up, s_fyr.at[0], to_y_up)
    share(far_down, s_x2.at[3])
    arrived(far_up, 0)
    share(far_up, s_x2.at[1])
    turn_corner(opposite - y, 2, 0)
    share_edge(opposite - y, 2)

    @pl.when(c == 0)
    def _():
        lax.fori_loop(0, 2, early_pass, 0)

    turn_corner(y_up - y, 1, 1)
    turn_corner(y_down - y, 3, 1)
    arrived(far_up, 1)
    push(far_up, 1, 12 + y_up - y_down, s_fyr.at[1], to_y_down)
    arrived(far_opposite, 0)
    share(far_opposite, s_x2.at[2])

    @pl.when(c == 0)
    def _():
        lax.fori_loop(2, 4, early_pass, 0)

    lax.fori_loop(0, 1, late_pass, 0)
    turn_corner(opposite - y, 2, 1)
    lax.fori_loop(0, 1, far_pass, 0)
    arrived(far_down, 1)
    lax.fori_loop(1, 2, late_pass, 0)
    arrived(far_opposite, 1)
    lax.fori_loop(1, 4, far_pass, 0)
    lax.fori_loop(2, 4, late_pass, 0)

    for part in (1 - k, k):
        start = pl.multiple_of((2 * part + 1 - c) * QUARTER, QUARTER)
        pltpu.make_async_remote_copy(
            src_ref=acc.at[pl.ds(start, QUARTER)],
            dst_ref=r1buf.at[part],
            send_sem=s_r1.at[part],
            recv_sem=r1_sem.at[part],
            device_id=other_core,
            device_id_type=MESH,
        ).start()

    def r1_arrived(part):
        pltpu.make_async_copy(r1buf.at[part], r1buf.at[part], r1_sem.at[part]).wait()

    away = pl.multiple_of((2 * (1 - k) + c) * QUARTER, QUARTER)
    r1_arrived(1 - k)
    r2src[...] = (acc[pl.ds(away, QUARTER), :] + r1buf[1 - k]).astype(r2src.dtype)
    cross = pltpu.make_async_remote_copy(
        src_ref=r2src,
        dst_ref=r2buf,
        send_sem=s_r2,
        recv_sem=r2_sem,
        device_id=to_rep,
        device_id_type=MESH,
    )
    cross.start()
    r1_arrived(k)
    home = pl.multiple_of((2 * k + c) * QUARTER, QUARTER)
    kept = acc[pl.ds(home, QUARTER), :] + r1buf[k]
    own = features.reshape(ROWS, WIDTH)[pl.ds(home, QUARTER), :]
    pre = jnp.dot(own, weight_self[...], preferred_element_type=jnp.float32)
    cross.wait()
    aggregate = (kept + r2buf[...].astype(jnp.float32)).astype(jnp.bfloat16)
    pre = pre + jnp.dot(aggregate, weight_neigh[...], preferred_element_type=jnp.float32)
    sigmoid = jax.nn.sigmoid(pre)
    out_ref[...] = (pre * sigmoid).astype(out_ref.dtype)
    slope = (cotangent[...].astype(jnp.float32) * sigmoid * (1.0 + pre * (1.0 - sigmoid))).astype(
        jnp.bfloat16
    )
    contract = (((0,), (0,)), ((), ()))
    self_term = lax.dot_general(own, slope, contract, preferred_element_type=jnp.float32)
    neigh_term = lax.dot_general(aggregate, slope, contract, preferred_element_type=jnp.float32)
    gsrc[...] = jnp.where(c == 0, neigh_term, self_term)
    core_swap = pltpu.make_async_remote_copy(
        src_ref=gsrc,
        dst_ref=gin,
        send_sem=s_g0,
        recv_sem=g0_sem,
        device_id=other_core,
        device_id_type=MESH,
    )
    core_swap.start()
    for part in range(2):
        pltpu.make_async_copy(r1buf.at[part], r1buf.at[part], s_r1.at[part]).wait()
    core_swap.wait()
    chip_term = jnp.where(c == 0, self_term, neigh_term) + gin[...]
    for side in range(2):
        gsum[:, side] = chip_term[:, side * TILE : (side + 1) * TILE].reshape(CHIPS // 2, 8, TILE)
    me = 32 * k + g

    def scatter(t, carry):
        peer = (me + t) % CHIPS
        pltpu.make_async_remote_copy(
            src_ref=gsum.at[peer // 2, peer % 2],
            dst_ref=rsbuf.at[t - 1],
            send_sem=s_rs,
            recv_sem=rs_sem,
            device_id=device(peer // 32, peer % 32, c),
            device_id_type=MESH,
        ).start()
        return carry

    lax.fori_loop(1, CHIPS, scatter, 0)
    everything = pltpu.make_async_copy(rsbuf, rsbuf, rs_sem)
    everything.wait()
    piece = gsum[me // 2, me % 2] + jnp.sum(rsbuf[...], axis=0)
    agbuf[me // 2, me % 2] = piece.astype(agbuf.dtype)

    def gather(t, carry):
        peer = (me + t) % CHIPS
        pltpu.make_async_remote_copy(
            src_ref=agbuf.at[me // 2, me % 2],
            dst_ref=agbuf.at[me // 2, me % 2],
            send_sem=s_ag,
            recv_sem=ag_sem,
            device_id=device(peer // 32, peer % 32, c),
            device_id_type=MESH,
        ).start()
        return carry

    lax.fori_loop(1, CHIPS, gather, 0)

    for n in range(3):
        sent(s_y.at[0, n], n)
        sent(s_y.at[1, n], n)
        sent(s_yr.at[n], n)
    for j in range(4):
        for n in range(2):
            sent(s_zd.at[j, n], n)
            sent(s_zu.at[j, n], n)

            @pl.when(turns(edge_high, (y + j) % 4 - y, j, n))
            def _():
                sent(s_t.at[j, n], n)

            sent(s_x.at[n, j], 0)
        sent(s_x2.at[j], 0)
    sent(s_rd, 0)
    sent(s_ru, 1)
    for n in range(2):
        sent(s_fy.at[0, n], n)
        sent(s_fy.at[1, n], n)
        sent(s_fyr.at[n], n)
    for step in range(STEPS):
        pltpu.make_async_copy(obuf.at[step], obuf.at[step], s_o.at[step]).wait()

    @pl.when(sender)
    def _():
        for number, start, size in cuts:
            here = fbuf.at[4, pl.ds(start, size)]
            pltpu.make_async_copy(here, here, s_swap.at[number]).wait()

    pltpu.make_async_copy(rsbuf, rsbuf, s_rs).wait()
    came_in = agbuf.reshape(CHIPS, 8, TILE).at[pl.ds(0, CHIPS - 1)]
    pltpu.make_async_copy(came_in, came_in, ag_sem).wait()
    last = pltpu.make_async_remote_copy(
        src_ref=agbuf,
        dst_ref=agother,
        send_sem=s_g1,
        recv_sem=g1_sem,
        device_id=other_core,
        device_id_type=MESH,
    )
    last.start()
    pltpu.make_async_copy(came_in, came_in, s_ag).wait()
    last.wait()
    held = agbuf[...].astype(jnp.float32)
    came = agother[...].astype(jnp.float32)
    self_ref[...] = jnp.where(c == 0, held, came)
    neigh_ref[...] = jnp.where(c == 0, came, held)


def finish_kernel(out_in, self_in, neigh_in, out_ref, self_ref, neigh_ref):
    out_ref[...] = out_in[...]
    for side in range(2):
        lanes = slice(side * TILE, (side + 1) * TILE)
        self_ref[:, lanes] = self_in[:, side].reshape(WIDTH, TILE)
        neigh_ref[:, lanes] = neigh_in[:, side].reshape(WIDTH, TILE)


def slot_table(rows, cols, counts):
    steps, slots = rows.shape
    key = rows * RT + cols
    live = jnp.arange(slots, dtype=jnp.int32)[None, :] < counts[:, None]
    number = jnp.arange(steps * slots, dtype=jnp.int32).reshape(steps, slots)
    hit = (key[:, None, :] == jnp.arange(RT * RT, dtype=jnp.int32)[None, :, None]) & live[:, None, :]
    found = jnp.max(jnp.where(hit, number[:, None, :], -1), axis=2)
    return jnp.where(found < 0, steps * slots, found).reshape(-1)


def on_device(
    features, tile_weights, tile_rows, tile_cols, tile_counts, weight_self, weight_neigh, cotangent
):
    table = slot_table(tile_rows[0, 0], tile_cols[0, 0], tile_counts[0, 0])
    weights = tile_weights.reshape(STEPS * SLOTS, TILE, TILE)
    vmem = pl.BlockSpec(memory_space=pltpu.VMEM)
    dma = pltpu.SemaphoreType.DMA
    raw = pl.pallas_call(
        aggregate_kernel,
        out_shape=(
            jax.ShapeDtypeStruct((QUARTER, WIDTH), jnp.bfloat16),
            jax.ShapeDtypeStruct((CHIPS // 2, 2, 8, TILE), jnp.float32),
            jax.ShapeDtypeStruct((CHIPS // 2, 2, 8, TILE), jnp.float32),
        ),
        in_specs=[
            pl.BlockSpec(memory_space=pltpu.SMEM),
            vmem,
            pl.BlockSpec(memory_space=pl.ANY),
            vmem,
            vmem,
            vmem,
        ],
        out_specs=(vmem, vmem, vmem),
        scratch_shapes=[
            pltpu.VMEM((STEPS * SLOTS + 1, TILE, TILE), jnp.bfloat16),
            pltpu.VMEM((2 * STEPS, HALF, WIDTH), jnp.bfloat16),
            pltpu.VMEM((STEPS, HALF, WIDTH), jnp.bfloat16),
            pltpu.VMEM((ROWS, WIDTH), jnp.float32),
            pltpu.VMEM((2, QUARTER, WIDTH), jnp.float32),
            pltpu.VMEM((QUARTER, WIDTH), jnp.bfloat16),
            pltpu.VMEM((QUARTER, WIDTH), jnp.bfloat16),
            dma((STEPS,)),
            dma((1,)),
            dma((2 * STEPS, 3)),
            dma((STEPS,)),
            dma((2,)),
            dma,
            dma((3,)),
            dma((2, 3)),
            dma((3,)),
            dma((4, 2)),
            dma((4, 2)),
            dma,
            dma,
            dma((2, 4)),
            dma((4,)),
            dma((STEPS,)),
            dma((2,)),
            dma,
            pltpu.VMEM((WIDTH, WIDTH), jnp.float32),
            pltpu.VMEM((WIDTH, WIDTH), jnp.float32),
            pltpu.VMEM((CHIPS // 2, 2, 8, TILE), jnp.float32),
            pltpu.VMEM((CHIPS - 1, 8, TILE), jnp.float32),
            pltpu.VMEM((CHIPS // 2, 2, 8, TILE), jnp.bfloat16),
            pltpu.VMEM((CHIPS // 2, 2, 8, TILE), jnp.bfloat16),
            dma,
            dma,
            dma,
            dma,
            dma,
            dma,
            dma,
            dma,
            pltpu.VMEM((4, HALF, WIDTH), jnp.bfloat16),
            dma((4, 2)),
            dma((4, 2)),
            dma((2, 2)),
            dma((2,)),
        ],
        compiler_params=pltpu.CompilerParams(
            collective_id=0, has_side_effects=True, vmem_limit_bytes=60 * 1024 * 1024
        ),
    )(
        table,
        features.reshape(2, HALF, WIDTH),
        weights,
        weight_self,
        weight_neigh,
        cotangent,
    )
    return pl.pallas_call(
        finish_kernel,
        out_shape=(
            jax.ShapeDtypeStruct((QUARTER, WIDTH), jnp.bfloat16),
            jax.ShapeDtypeStruct((WIDTH, WIDTH), jnp.float32),
            jax.ShapeDtypeStruct((WIDTH, WIDTH), jnp.float32),
        ),
        in_specs=[vmem, vmem, vmem],
        out_specs=(vmem, vmem, vmem),
    )(*raw)


def solution(mesh):
    return jax.shard_map(
        on_device,
        mesh=mesh,
        in_specs=(
            P("dom", None),
            P("dom", "rep", None, None, None, None),
            P("dom", "rep", None, None),
            P("dom", "rep", None, None),
            P("dom", "rep", None),
            P(),
            P(),
            P(("dom", "rep"), None),
        ),
        out_specs=(P(("dom", "rep"), None), P(), P()),
        check_vma=False,
    )
```

time: 122 us -> 113 us (0.926)
  Pallas kernels: 114 us -> 109 us
  local copies, waits for them, and re-layouts: 5.03 us -> 0.08 us
    pallas_call x1, Pallas kernels: 114 us -> 107 us  [on_device(): pl.pallas_call(aggregate_kernel, out_shape=(jax.ShapeDtypeStruct((QUARTER...]
    unnamed x3 -> x0, local copies, waits for them, and re-layouts: 4.95 us -> none
    pallas_call x0 -> x1, Pallas kernels: none -> 2 us  [on_device(): pl.pallas_call(finish_kernel, out_shape=(jax.ShapeDtypeStruct((QUARTER, W...]
where the time goes in v3:
time: 113 us; the launch traced here: 112 us
  Pallas kernels  109 us (96%)
  other arithmetic  2.41 us (2%)
    pallas_call x1, Pallas kernels, on_device(): pl.pallas_call(aggregate_kernel, out_shape=(jax.ShapeDtypeStruct((QUARTER...  107 us

profile of v3, /device:TPU:1, one launch (start us, length us, event | category | flops | bytes accessed | tf_op | source)
XLA Modules:
  0.0 112.4 jit_solution(17804983856710192440)
XLA Ops:
  0.6 0.7 iota_compare_fusion.1
  1.4 0.7 add_bitcast_fusion
  2.1 0.4 select_reduce_fusion
  2.4 0.1 reduce_max.12
  2.5 0.6 compare_select_fusion.slots
  3.1 107.3 %shard_map.103 = (bf16[384,256]{1,0:T(8,128)(2,1)}, f32[32,2,8,128]{3,2,1,0:T(8,128)}, f32[32,2,8,128]{3,2,1,0:T(8,128)}) custom-call(s32[1152]{0:T(1024)} %compare_select_fusion.slots, bf16[2,768,256]{2,1,0:T(8,128)(2,1)} %bitcast.6, bf16[704,128,128]{2,1,0:T(8,128)(2,1)} %bitcast.5, bf16[256,256]{1,0:T(8,128)(2,1)} %weight_self.1, ...), custom_call_target="tpu_custom_call" | custom-call | tf_op jit(solution)/shard_map/pallas_call | solution.py:598
  110.4 2.0 %shard_map.104 = (bf16[384,256]{1,0:T(8,128)(2,1)}, f32[256,256]{1,0:T(8,128)}, f32[256,256]{1,0:T(8,128)}) custom-call(bf16[384,256]{1,0:T(8,128)(2,1)} %get-tuple-element.6.out_in, f32[32,2,8,128]{3,2,1,0:T(8,128)} %get-tuple-element.7.self_in, f32[32,2,8,128]{3,2,1,0:T(8,128)} %get-tuple-element.8.neigh_in), custom_call_target="tpu_custom_call" | custom-call | tf_op jit(solution)/shard_map/pallas_call | solution.py:671
  (1 shorter events, 0.0 us)

commit v4 on v3

--- a/solution.py
+++ b/solution.py
@@ -37,7 +37,9 @@
 
 
 def aggregate_kernel(
-    slots,
+    counts,
+    tile_rows,
+    tile_cols,
     features,
     weights,
     weight_self,
@@ -90,6 +92,9 @@
     s_t,
     s_fy,
     s_fyr,
+    table,
+    slots,
+    table_sem,
 ):
     k, c, g = where_am_i()
     z, y = g // 4, g % 4
@@ -167,7 +172,7 @@
     cuts = ((0, 0, EDGE), (1, EDGE, EDGE), (2, 2 * EDGE, COMMON))
 
     def swap(target):
-        for number, start, size in cuts:
+        for number, start, size in (cuts[1], cuts[2], cuts[0]):
             pltpu.make_async_remote_copy(
                 src_ref=features.at[c, pl.ds(start, size)],
                 dst_ref=fbuf.at[4, pl.ds(start, size)],
@@ -261,6 +266,20 @@
     @pl.when(c == 1)
     def _():
         give_core(4)
+
+    shape = (RT * RT, SLOTS)
+    places = lax.broadcasted_iota(jnp.int32, shape, 0)
+    numbers = lax.broadcasted_iota(jnp.int32, shape, 1)
+    lanes = lax.broadcasted_iota(jnp.int32, (RT * RT, TILE), 1)
+    found = jnp.full((RT * RT, TILE), STEPS * SLOTS, jnp.int32)
+    for step in range(STEPS):
+        names = tile_rows[step : step + 1, :] * RT + tile_cols[step : step + 1, :]
+        hit = jnp.logical_and(names == places, numbers < counts[0, step])
+        best = jnp.min(jnp.where(hit, numbers + step * SLOTS, STEPS * SLOTS), axis=1, keepdims=True)
+        found = jnp.where(lanes == step, best, found)
+    table[...] = found
+    table_copy = pltpu.make_async_copy(table, slots, table_sem)
+    table_copy.start()
 
     from_up = 4 + y_up - y
     from_down = 4 + y_down - y
@@ -322,6 +341,7 @@
     share_edge(y_down - y, 3)
 
     acc[...] = jnp.zeros_like(acc)
+    table_copy.wait()
     for step in range(STEPS):
         pltpu.make_async_copy(
             weights.at[pl.ds(step * SLOTS, SLOTS)], wbuf.at[pl.ds(step * SLOTS, SLOTS)], w_sem.at[step]
@@ -335,13 +355,13 @@
         half_cols = RT // 2
 
         def rows_of(r, carry):
-            base = step * (RT * RT) + r * (group * RT)
+            base = r * (group * RT)
             total = None
             for ref, at_slot, side in ((fbuf, slot, c), (obuf, step, 1 - c)):
                 stacked = []
                 for n in range(group):
                     tiles = [
-                        wbuf[slots[base + n * RT + half_cols * side + i]] for i in range(half_cols)
+                        wbuf[slots[base + n * RT + half_cols * side + i, step]] for i in range(half_cols)
                     ]
                     stacked.append(jnp.concatenate(tiles, axis=1))
                 lhs = jnp.concatenate(stacked, axis=0)
@@ -578,20 +598,9 @@
         neigh_ref[:, lanes] = neigh_in[:, side].reshape(WIDTH, TILE)
 
 
-def slot_table(rows, cols, counts):
-    steps, slots = rows.shape
-    key = rows * RT + cols
-    live = jnp.arange(slots, dtype=jnp.int32)[None, :] < counts[:, None]
-    number = jnp.arange(steps * slots, dtype=jnp.int32).reshape(steps, slots)
-    hit = (key[:, None, :] == jnp.arange(RT * RT, dtype=jnp.int32)[None, :, None]) & live[:, None, :]
-    found = jnp.max(jnp.where(hit, number[:, None, :], -1), axis=2)
-    return jnp.where(found < 0, steps * slots, found).reshape(-1)
-
-
 def on_device(
     features, tile_weights, tile_rows, tile_cols, tile_counts, weight_self, weight_neigh, cotangent
 ):
-    table = slot_table(tile_rows[0, 0], tile_cols[0, 0], tile_counts[0, 0])
     weights = tile_weights.reshape(STEPS * SLOTS, TILE, TILE)
     vmem = pl.BlockSpec(memory_space=pltpu.VMEM)
     dma = pltpu.SemaphoreType.DMA
@@ -604,6 +613,8 @@
         ),
         in_specs=[
             pl.BlockSpec(memory_space=pltpu.SMEM),
+            vmem,
+            vmem,
             vmem,
             pl.BlockSpec(memory_space=pl.ANY),
             vmem,
@@ -656,12 +667,17 @@
             dma((4, 2)),
             dma((2, 2)),
             dma((2,)),
+            pltpu.VMEM((RT * RT, TILE), jnp.int32),
+            pltpu.SMEM((RT * RT, TILE), jnp.int32),
+            dma,
         ],
         compiler_params=pltpu.CompilerParams(
             collective_id=0, has_side_effects=True, vmem_limit_bytes=60 * 1024 * 1024
         ),
     )(
-        table,
+        tile_counts.reshape(1, STEPS),
+        tile_rows.reshape(STEPS, SLOTS),
+        tile_cols.reshape(STEPS, SLOTS),
         features.reshape(2, HALF, WIDTH),
         weights,
         weight_self,

time: 113 us -> 110 us (0.973)
  other arithmetic: 2.41 us -> 0 us
where the time goes in v4:
time: 110 us
  Pallas kernels  109 us (99%)
    pallas_call x1, Pallas kernels, on_device(): pl.pallas_call(aggregate_kernel, out_shape=(jax.ShapeDtypeStruct((QUARTER...  107 us

profile of v4, /device:TPU:1, one launch (start us, length us, event | category | flops | bytes accessed | tf_op | source)
XLA Modules:
  0.0 109.5 jit_solution(17231248886342044899)
XLA Ops:
  0.6 106.9 %shard_map.103 = (bf16[384,256]{1,0:T(8,128)(2,1)}, f32[32,2,8,128]{3,2,1,0:T(8,128)}, f32[32,2,8,128]{3,2,1,0:T(8,128)}) custom-call(s32[1,8]{1,0:T(1,128)} %bitcast.9, s32[8,88]{1,0:T(8,128)} %bitcast.7, s32[8,88]{1,0:T(8,128)} %bitcast.8, bf16[2,768,256]{2,1,0:T(8,128)(2,1)} %bitcast.6, bf16[704,128,128]{2,1,0:T(8,128)(2,1)} %bitcast.5, ...), custom_call_target="tpu_custom_call" | custom-call | tf_op jit(solution)/shard_map/pallas_call | solution.py:607
  107.6 2.0 %shard_map.104 = (bf16[384,256]{1,0:T(8,128)(2,1)}, f32[256,256]{1,0:T(8,128)}, f32[256,256]{1,0:T(8,128)}) custom-call(bf16[384,256]{1,0:T(8,128)(2,1)} %get-tuple-element.6.out_in, f32[32,2,8,128]{3,2,1,0:T(8,128)} %get-tuple-element.7.self_in, f32[32,2,8,128]{3,2,1,0:T(8,128)} %get-tuple-element.8.neigh_in), custom_call_target="tpu_custom_call" | custom-call | tf_op jit(solution)/shard_map/pallas_call | solution.py:687
